TPU v7x, 256 devices: a whole 4x4x8 slice. The times are simulated.
256 devices in a mesh: peer: 8 (over x, y_hi), space: 32 (over y_lo, z, core).
Axes of the slice: x: 4, y: 4 (y_hi: 2, y_lo: 2; y = y_hi * 2 + y_lo), z: 8, core: 2. Of those that a mesh axis runs over, the one named last changes fastest.
Arguments:
- images: bfloat16 [8, 512, 32, 512], P('peer', 'space'), may hold values from -6 to 6
- task_grad: bfloat16 [8, 512, 32, 512], P('peer', 'space'), may hold values from -6 to 6
- pairing: int32 [8], replicated, may hold values from 0 to 7, as said below
- first_kernel: bfloat16 [8, 3, 3, 512, 512], P('peer'), may hold values from -0.09375 to 0.09375
- first_scale: float32 [8, 512], P('peer'), may hold values from 0.25 to 1.75
- first_shift: float32 [8, 512], P('peer'), may hold values from -3 to 3
- second_kernel: bfloat16 [8, 3, 3, 512, 512], P('peer'), may hold values from -0.09375 to 0.09375
- second_scale: float32 [8, 512], P('peer'), may hold values from 0.25 to 1.75
- second_shift: float32 [8, 512], P('peer'), may hold values from -3 to 3
Outputs:
- input_grad: bfloat16 [8, 512, 32, 512], P('peer', 'space')
Inputs may be any that keep to these rules, and one draw needn't show every extreme that they name: `pairing`: every network index appears exactly once.
All inputs are finite; a program needn't handle non-finite values.
Results may differ from a plain program's by a relative error of at most 0.012.
Values may be sent and summed in bfloat16 or wider, within the bound.
A program may use at most 64 MiB of HBM per device.

v0:
```python
import jax
import jax.numpy as jnp
from jax import lax
from jax.sharding import PartitionSpec as P


def extended(cells, sides, width):
    for axis, dim in sides:
        count = lax.axis_size(axis)
        ends = count - 1
        head = lax.slice_in_dim(cells, 0, width, axis=dim)
        tail = lax.slice_in_dim(cells, cells.shape[dim] - width, cells.shape[dim], axis=dim)
        cells = jnp.concatenate(
            [
                lax.ppermute(tail, axis, [(i, (i + 1) % count) for i in range(ends)]),
                cells,
                lax.ppermute(head, axis, [((i + 1) % count, i) for i in range(ends)]),
            ],
            axis=dim,
        )
    return cells


def apply_dilated_filter(
    padded_row_count, filter_kernel, dilation_rate, output_rows, reverse_kernel
):
    input_width = padded_row_count.shape[1]
    padded_input = jnp.pad(padded_row_count, ((0, 0), (dilation_rate, dilation_rate), (0, 0)))
    total = jnp.zeros((output_rows, input_width, filter_kernel.shape[2]), jnp.float32)
    for kernel_tap_row in range(3):
        for kernel_tap_column in range(3):
            input_window = padded_input[
                kernel_tap_row * dilation_rate : kernel_tap_row * dilation_rate + output_rows,
                kernel_tap_column * dilation_rate : kernel_tap_column * dilation_rate + input_width,
            ]
            if reverse_kernel:
                total = total + jnp.einsum(
                    "rwo,io->rwi",
                    input_window,
                    filter_kernel[2 - kernel_tap_row, 2 - kernel_tap_column],
                    preferred_element_type=jnp.float32,
                )
            else:
                total = total + jnp.einsum(
                    "rwi,io->rwo",
                    input_window,
                    filter_kernel[kernel_tap_row, kernel_tap_column],
                    preferred_element_type=jnp.float32,
                )
    return total


def silu_slope(value):
    sig = jax.nn.sigmoid(value)
    return sig * (1.0 + value * (1.0 - sig))


def per_device(
    images,
    task_grad,
    pairing,
    first_kernel,
    first_scale,
    first_shift,
    second_kernel,
    second_scale,
    second_shift,
):
    image = images[0]
    strip_rows = image.shape[0]
    kernel_one = first_kernel[0]
    kernel_two = second_kernel[0]
    scale_one = first_scale[0]
    shift_one = first_shift[0]
    scale_two = second_scale[0]
    shift_two = second_shift[0]
    image_ext = extended(image, (("space", 0),), 2)
    pre_first = (
        scale_one * apply_dilated_filter(image_ext, kernel_one, 2, strip_rows, False) + shift_one
    )
    hidden = jax.nn.silu(pre_first).astype(jnp.bfloat16)
    hidden_ext = extended(hidden, (("space", 0),), 4)
    pre_second = (
        scale_two * apply_dilated_filter(hidden_ext, kernel_two, 4, strip_rows, False) + shift_two
    )
    feat = jax.nn.silu(pre_second).astype(jnp.bfloat16)
    partner = pairing[lax.axis_index("peer")]
    piece = lax.all_gather(feat[None], "peer", axis=0, tiled=True)
    owners = jnp.arange(piece.shape[0], dtype=jnp.int32)
    pick = (owners == partner).astype(jnp.bfloat16)
    partner_feat = jnp.einsum("k,krwc->rwc", pick, piece, preferred_element_type=jnp.float32)
    cot = task_grad[0].astype(jnp.float32) + feat.astype(jnp.float32) - partner_feat
    grad_second = (cot * silu_slope(pre_second) * scale_two).astype(jnp.bfloat16)
    grad_second_ext = extended(grad_second, (("space", 0),), 4)
    grad_hidden = apply_dilated_filter(grad_second_ext, kernel_two, 4, strip_rows, True)
    grad_first = (grad_hidden * silu_slope(pre_first) * scale_one).astype(jnp.bfloat16)
    grad_first_ext = extended(grad_first, (("space", 0),), 2)
    input_grad = apply_dilated_filter(grad_first_ext, kernel_one, 2, strip_rows, True).astype(
        jnp.bfloat16
    )
    return input_grad[None]


def solution(mesh):
    placed = (
        P("peer", "space", None, None),
        P("peer", "space", None, None),
        P(),
        P("peer", None, None, None, None),
        P("peer", None),
        P("peer", None),
        P("peer", None, None, None, None),
        P("peer", None),
        P("peer", None),
    )
    return jax.shard_map(
        per_device,
        mesh=mesh,
        in_specs=placed,
        out_specs=P("peer", "space", None, None),
        check_vma=False,
    )
```

profile of v0, /device:TPU:8, one launch (start us, length us, event | category | flops | bytes accessed | tf_op | source)
XLA Modules:
  0.0 162.6 jit_solution(12028353491544414029)
XLA Ops:
  6.5 1.0 slice_bitcast_fusion.55
  7.6 2.1 %collective-permute-start = (bf16[2,32,512]{2,1,0:T(8,128)(2,1)S(1)}, bf16[2,32,512]{2,1,0:T(8,128)(2,1)S(1)}, u32[]{:S(2)}, u32[]{:S(2)}) collective-permute-start(bf16[2,32,512]{2,1,0:T(8,128)(2,1)S(1)} %get-tuple-element.11), channel_id=1, source_target_pairs={{0,1},{1,2},{2,3},{3,4},{4,5},{5,6},{6,7},{7,8},{8,9},{9,10},{10,1... | collective-permute-start | bytes 196616 | tf_op jit(solution)/shard_map/ppermute | solution.py:15
  9.6 7.1 %collective-permute-start.1 = (bf16[2,32,512]{2,1,0:T(8,128)(2,1)S(1)}, bf16[2,32,512]{2,1,0:T(8,128)(2,1)S(1)}, u32[]{:S(2)}, u32[]{:S(2)}) collective-permute-start(bf16[2,32,512]{2,1,0:T(8,128)(2,1)S(1)} %get-tuple-element.12), channel_id=1, source_target_pairs={{1,0},{2,1},{3,2},{4,3},{5,4},{6,5},{7,6},{8,7},{9,8},{10,9},{11,1... | collective-permute-start | bytes 196616 | tf_op jit(solution)/shard_map/ppermute | solution.py:17
  16.7 0.0 collective-permute-done
  16.7 1.9 %collective-permute-done.1 = bf16[2,32,512]{2,1,0:T(8,128)(2,1)S(1)} collective-permute-done((bf16[2,32,512]{2,1,0:T(8,128)(2,1)S(1)}, bf16[2,32,512]{2,1,0:T(8,128)(2,1)S(1)}, u32[]{:S(2)}, u32[]{:S(2)}) %collective-permute-start.1) | collective-permute-done | bytes 65568 | tf_op jit(solution)/shard_map/ppermute | solution.py:17
  18.6 1.4 fusion.30
  20.0 1.5 fusion.80
  21.5 1.6 fusion.45
  23.1 0.4 convolution_add_fusion.27
  23.6 0.5 convolution_add_fusion.26
  24.0 0.4 convolution_add_fusion.25
  24.5 0.4 convolution_add_fusion.24
  24.9 0.5 convolution_add_fusion.23
  25.4 0.4 convolution_add_fusion.22
  25.9 0.0 slice-start.1
  25.9 0.7 multiply_convert_fusion.1
  26.6 2.1 %collective-permute-start.2 = (bf16[4,32,512]{2,1,0:T(8,128)(2,1)S(1)}, bf16[4,32,512]{2,1,0:T(8,128)(2,1)S(1)}, u32[]{:S(2)}, u32[]{:S(2)}) collective-permute-start(bf16[4,32,512]{2,1,0:T(8,128)(2,1)S(1)} %get-tuple-element.9), channel_id=1, source_target_pairs={{0,1},{1,2},{2,3},{3,4},{4,5},{5,6},{6,7},{7,8},{8,9},{9,10},{10,1... | collective-permute-start | bytes 393224 | tf_op jit(solution)/shard_map/ppermute | solution.py:15
  28.6 5.8 %collective-permute-start.3 = (bf16[4,32,512]{2,1,0:T(8,128)(2,1)S(1)}, bf16[4,32,512]{2,1,0:T(8,128)(2,1)S(1)}, u32[]{:S(2)}, u32[]{:S(2)}) collective-permute-start(bf16[4,32,512]{2,1,0:T(8,128)(2,1)S(1)} %get-tuple-element.10), channel_id=1, source_target_pairs={{1,0},{2,1},{3,2},{4,3},{5,4},{6,5},{7,6},{8,7},{9,8},{10,9},{11,1... | collective-permute-start | bytes 393224 | tf_op jit(solution)/shard_map/ppermute | solution.py:17
  34.5 0.7 collective-permute-done.2
  35.2 1.8 %collective-permute-done.3 = bf16[4,32,512]{2,1,0:T(8,128)(2,1)S(1)} collective-permute-done((bf16[4,32,512]{2,1,0:T(8,128)(2,1)S(1)}, bf16[4,32,512]{2,1,0:T(8,128)(2,1)S(1)}, u32[]{:S(2)}, u32[]{:S(2)}) %collective-permute-start.3) | collective-permute-done | bytes 131104 | tf_op jit(solution)/shard_map/ppermute | solution.py:17
  37.0 0.5 fusion.25
  37.4 0.4 fusion.73
  37.9 0.4 fusion.31
  38.3 0.4 convolution_add_fusion.21
  38.8 0.4 convolution_add_fusion.20
  39.2 0.4 convolution_add_fusion.19
  39.7 0.4 convolution_add_fusion.18
  40.1 0.4 convolution_add_fusion.17
  40.6 0.4 convolution_add_fusion.16
  41.0 0.0 slice-start.2
  41.1 1.5 multiply_convert_fusion
  42.5 0.0 all-gather.3.cloned.1.call-update
  42.6 0.6 dynamic_slice.3
  43.2 75.5 %all-gather.3.cloned.1.call-done = bf16[128,32,512]{2,1,0:T(8,128)(2,1)} async-done(((bf16[16,32,512]{2,1,0:T(8,128)(2,1)}), bf16[128,32,512]{2,1,0:T(8,128)(2,1)}) %all-gather.3.cloned.1.call-update) | async-done | bytes 4194320 | tf_op jit(solution)/shard_map/all_gather | solution.py:88
  118.7 5.9 %fusion = f32[1,16,32,512]{3,0,2,1:T(1,128)S(1)} fusion(bf16[8,16,32,512]{3,2,1,0:T(8,128)(2,1)} %bitcast.184, s32[]{:T(128)} %bitcast.46), kind=kOutput, calls=%fused_computation | convolution fusion | flops 4194312 | bytes 5242884 | tf_op jit(solution)/shard_map/k,krwc->rwc/dot_general | solution.py:91
  124.6 0.6 fusion.20
  125.2 1.9 %collective-permute-start.4 = (bf16[4,32,512]{2,1,0:T(8,128)(2,1)S(1)}, bf16[4,32,512]{2,1,0:T(8,128)(2,1)S(1)}, u32[]{:S(2)}, u32[]{:S(2)}) collective-permute-start(bf16[4,32,512]{2,1,0:T(8,128)(2,1)S(1)} %get-tuple-element.7), channel_id=1, source_target_pairs={{0,1},{1,2},{2,3},{3,4},{4,5},{5,6},{6,7},{7,8},{8,9},{9,10},{10,1... | collective-permute-start | bytes 393224 | tf_op jit(solution)/shard_map/ppermute | solution.py:15
  127.1 5.9 %collective-permute-start.5 = (bf16[4,32,512]{2,1,0:T(8,128)(2,1)S(1)}, bf16[4,32,512]{2,1,0:T(8,128)(2,1)S(1)}, u32[]{:S(2)}, u32[]{:S(2)}) collective-permute-start(bf16[4,32,512]{2,1,0:T(8,128)(2,1)S(1)} %get-tuple-element.8), channel_id=1, source_target_pairs={{1,0},{2,1},{3,2},{4,3},{5,4},{6,5},{7,6},{8,7},{9,8},{10,9},{11,1... | collective-permute-start | bytes 393224 | tf_op jit(solution)/shard_map/ppermute | solution.py:17
  133.1 0.5 collective-permute-done.4
  133.6 1.8 %collective-permute-done.5 = bf16[4,32,512]{2,1,0:T(8,128)(2,1)S(1)} collective-permute-done((bf16[4,32,512]{2,1,0:T(8,128)(2,1)S(1)}, bf16[4,32,512]{2,1,0:T(8,128)(2,1)S(1)}, u32[]{:S(2)}, u32[]{:S(2)}) %collective-permute-start.5) | collective-permute-done | bytes 131104 | tf_op jit(solution)/shard_map/ppermute | solution.py:17
  135.4 0.5 select_maximum_fusion
  135.9 0.5 fusion.66
  136.3 0.5 fusion.38
  136.8 0.5 convolution_add_fusion.15
  137.3 0.5 convolution_add_fusion.14
  137.8 0.5 convolution_add_fusion.13
  138.2 0.5 convolution_add_fusion.12
  138.7 0.5 convolution_add_fusion.11
  139.2 0.5 convolution_add_fusion.10
  139.7 0.7 fusion.15
  140.5 2.1 %collective-permute-start.6 = (bf16[2,32,512]{2,1,0:T(8,128)(2,1)S(1)}, bf16[2,32,512]{2,1,0:T(8,128)(2,1)S(1)}, u32[]{:S(2)}, u32[]{:S(2)}) collective-permute-start(bf16[2,32,512]{2,1,0:T(8,128)(2,1)S(1)} %get-tuple-element.5), channel_id=1, source_target_pairs={{0,1},{1,2},{2,3},{3,4},{4,5},{5,6},{6,7},{7,8},{8,9},{9,10},{10,1... | collective-permute-start | bytes 196616 | tf_op jit(solution)/shard_map/ppermute | solution.py:15
  142.5 5.9 %collective-permute-start.7 = (bf16[2,32,512]{2,1,0:T(8,128)(2,1)S(1)}, bf16[2,32,512]{2,1,0:T(8,128)(2,1)S(1)}, u32[]{:S(2)}, u32[]{:S(2)}) collective-permute-start(bf16[2,32,512]{2,1,0:T(8,128)(2,1)S(1)} %get-tuple-element.6), channel_id=1, source_target_pairs={{1,0},{2,1},{3,2},{4,3},{5,4},{6,5},{7,6},{8,7},{9,8},{10,9},{11,1... | collective-permute-start | bytes 196616 | tf_op jit(solution)/shard_map/ppermute | solution.py:17
  148.4 0.0 collective-permute-done.6
  148.4 1.9 %collective-permute-done.7 = bf16[2,32,512]{2,1,0:T(8,128)(2,1)S(1)} collective-permute-done((bf16[2,32,512]{2,1,0:T(8,128)(2,1)S(1)}, bf16[2,32,512]{2,1,0:T(8,128)(2,1)S(1)}, u32[]{:S(2)}, u32[]{:S(2)}) %collective-permute-start.7) | collective-permute-done | bytes 65568 | tf_op jit(solution)/shard_map/ppermute | solution.py:17
  150.3 0.3 select_maximum_fusion.2
  150.7 0.5 fusion.59
  151.2 0.5 fusion.52
  151.6 0.5 convolution_add_fusion.9
  152.1 0.5 convolution_add_fusion.8
  152.6 0.5 convolution_add_fusion.7
  153.1 0.5 convolution_add_fusion.6
  153.5 0.5 convolution_add_fusion.5
  154.0 0.5 convolution_add_fusion.4
  154.5 1.3 fusion.16
  (33 shorter events, 0.1 us)
Async XLA Ops:
  6.5 112.2 %all-gather.3.cloned.1.call-start = ((), (), s32[]{:S(2)}) async-start(), calls=%async_computation | async-start | bytes 4718592 | tf_op jit(solution)/shard_map/all_gather | solution.py:88
  6.5 16.6 %copy-start = (bf16[1,3,3,512,512]{4,3,2,1,0:T(8,128)(2,1)S(1)}, bf16[1,3,3,512,512]{4,3,2,1,0:T(8,128)(2,1)}, u32[]{:S(2)}) copy-start(bf16[1,3,3,512,512]{4,3,2,1,0:T(8,128)(2,1)} %param.12) | copy-start | bytes 14155780
  7.6 9.2 %collective-permute-start = (bf16[2,32,512]{2,1,0:T(8,128)(2,1)S(1)}, bf16[2,32,512]{2,1,0:T(8,128)(2,1)S(1)}, u32[]{:S(2)}, u32[]{:S(2)}) collective-permute-start(bf16[2,32,512]{2,1,0:T(8,128)(2,1)S(1)} %get-tuple-element.11), channel_id=1, source_target_pairs={{0,1},{1,2},{2,3},{3,4},{4,5},{5,6},{6,7},{7,8},{8,9},{9,10},{10,1... | collective-permute-start | bytes 196616 | tf_op jit(solution)/shard_map/ppermute | solution.py:15
  9.6 9.0 %collective-permute-start.1 = (bf16[2,32,512]{2,1,0:T(8,128)(2,1)S(1)}, bf16[2,32,512]{2,1,0:T(8,128)(2,1)S(1)}, u32[]{:S(2)}, u32[]{:S(2)}) collective-permute-start(bf16[2,32,512]{2,1,0:T(8,128)(2,1)S(1)} %get-tuple-element.12), channel_id=1, source_target_pairs={{1,0},{2,1},{3,2},{4,3},{5,4},{6,5},{7,6},{8,7},{9,8},{10,9},{11,1... | collective-permute-start | bytes 196616 | tf_op jit(solution)/shard_map/ppermute | solution.py:17
  23.1 1.4 copy-start.1
  24.5 1.4 copy-start.4
  24.5 1.4 copy-start.6
  25.4 12.0 %slice-start = ((s8[4718592]{0:T(1024)(128)(4,1)}), s8[4194304]{0:T(1024)(128)(4,1)S(1)}, s32[]{:S(2)}) async-start(s8[4718592]{0:T(1024)(128)(4,1)} %bitcast.142), calls=%async_computation.1 | async-start | bytes 8388608
  25.9 11.6 %slice-start.1 = ((s8[4718592]{0:T(1024)(128)(4,1)}), s8[524288]{0:T(1024)(128)(4,1)S(1)}, s32[]{:S(2)}) async-start(s8[4718592]{0:T(1024)(128)(4,1)} %bitcast.142), calls=%async_computation.2 | async-start | bytes 1048576
  26.6 8.6 %collective-permute-start.2 = (bf16[4,32,512]{2,1,0:T(8,128)(2,1)S(1)}, bf16[4,32,512]{2,1,0:T(8,128)(2,1)S(1)}, u32[]{:S(2)}, u32[]{:S(2)}) collective-permute-start(bf16[4,32,512]{2,1,0:T(8,128)(2,1)S(1)} %get-tuple-element.9), channel_id=1, source_target_pairs={{0,1},{1,2},{2,3},{3,4},{4,5},{5,6},{6,7},{7,8},{8,9},{9,10},{10,1... | collective-permute-start | bytes 393224 | tf_op jit(solution)/shard_map/ppermute | solution.py:15
  28.6 8.3 %collective-permute-start.3 = (bf16[4,32,512]{2,1,0:T(8,128)(2,1)S(1)}, bf16[4,32,512]{2,1,0:T(8,128)(2,1)S(1)}, u32[]{:S(2)}, u32[]{:S(2)}) collective-permute-start(bf16[4,32,512]{2,1,0:T(8,128)(2,1)S(1)} %get-tuple-element.10), channel_id=1, source_target_pairs={{1,0},{2,1},{3,2},{4,3},{5,4},{6,5},{7,6},{8,7},{9,8},{10,9},{11,1... | collective-permute-start | bytes 393224 | tf_op jit(solution)/shard_map/ppermute | solution.py:17
  39.7 1.4 copy-start.3
  39.7 1.4 copy-start.5
  41.0 1.5 copy-start.7
  41.0 94.8 %slice-start.2 = ((s8[4718592]{0:T(1024)(128)(4,1)}), s8[524288]{0:T(1024)(128)(4,1)S(1)}, s32[]{:S(2)}) async-start(s8[4718592]{0:T(1024)(128)(4,1)} %bitcast.153), calls=%async_computation.3 | async-start | bytes 1048576
  42.5 82.1 %copy-start.2 = (bf16[1,16,32,512]{3,2,1,0:T(8,128)(2,1)S(1)}, bf16[1,16,32,512]{3,2,1,0:T(8,128)(2,1)}, u32[]{:S(2)}) copy-start(bf16[1,16,32,512]{3,2,1,0:T(8,128)(2,1)} %param.10) | copy-start | bytes 1572868
  118.7 17.2 %slice-start.3 = ((s8[4718592]{0:T(1024)(128)(4,1)}), s8[4194304]{0:T(1024)(128)(4,1)S(1)}, s32[]{:S(2)}) async-start(s8[4718592]{0:T(1024)(128)(4,1)} %bitcast.153), calls=%async_computation.4 | async-start | bytes 8388608
  125.2 8.4 %collective-permute-start.4 = (bf16[4,32,512]{2,1,0:T(8,128)(2,1)S(1)}, bf16[4,32,512]{2,1,0:T(8,128)(2,1)S(1)}, u32[]{:S(2)}, u32[]{:S(2)}) collective-permute-start(bf16[4,32,512]{2,1,0:T(8,128)(2,1)S(1)} %get-tuple-element.7), channel_id=1, source_target_pairs={{0,1},{1,2},{2,3},{3,4},{4,5},{5,6},{6,7},{7,8},{8,9},{9,10},{10,1... | collective-permute-start | bytes 393224 | tf_op jit(solution)/shard_map/ppermute | solution.py:15
  127.1 8.3 %collective-permute-start.5 = (bf16[4,32,512]{2,1,0:T(8,128)(2,1)S(1)}, bf16[4,32,512]{2,1,0:T(8,128)(2,1)S(1)}, u32[]{:S(2)}, u32[]{:S(2)}) collective-permute-start(bf16[4,32,512]{2,1,0:T(8,128)(2,1)S(1)} %get-tuple-element.8), channel_id=1, source_target_pairs={{1,0},{2,1},{3,2},{4,3},{5,4},{6,5},{7,6},{8,7},{9,8},{10,9},{11,1... | collective-permute-start | bytes 393224 | tf_op jit(solution)/shard_map/ppermute | solution.py:17
  139.2 11.4 %slice-start.4 = ((s8[4718592]{0:T(1024)(128)(4,1)}), s8[524288]{0:T(1024)(128)(4,1)S(1)}, s32[]{:S(2)}) async-start(s8[4718592]{0:T(1024)(128)(4,1)} %bitcast.173), calls=%async_computation.5 | async-start | bytes 1048576
  139.7 11.0 %slice-start.5 = ((s8[4718592]{0:T(1024)(128)(4,1)}), s8[4194304]{0:T(1024)(128)(4,1)S(1)}, s32[]{:S(2)}) async-start(s8[4718592]{0:T(1024)(128)(4,1)} %bitcast.173), calls=%async_computation.6 | async-start | bytes 8388608
  140.5 8.0 %collective-permute-start.6 = (bf16[2,32,512]{2,1,0:T(8,128)(2,1)S(1)}, bf16[2,32,512]{2,1,0:T(8,128)(2,1)S(1)}, u32[]{:S(2)}, u32[]{:S(2)}) collective-permute-start(bf16[2,32,512]{2,1,0:T(8,128)(2,1)S(1)} %get-tuple-element.5), channel_id=1, source_target_pairs={{0,1},{1,2},{2,3},{3,4},{4,5},{5,6},{6,7},{7,8},{8,9},{9,10},{10,1... | collective-permute-start | bytes 196616 | tf_op jit(solution)/shard_map/ppermute | solution.py:15
  142.5 7.8 %collective-permute-start.7 = (bf16[2,32,512]{2,1,0:T(8,128)(2,1)S(1)}, bf16[2,32,512]{2,1,0:T(8,128)(2,1)S(1)}, u32[]{:S(2)}, u32[]{:S(2)}) collective-permute-start(bf16[2,32,512]{2,1,0:T(8,128)(2,1)S(1)} %get-tuple-element.6), channel_id=1, source_target_pairs={{1,0},{2,1},{3,2},{4,3},{5,4},{6,5},{7,6},{8,7},{9,8},{10,9},{11,1... | collective-permute-start | bytes 196616 | tf_op jit(solution)/shard_map/ppermute | solution.py:17
Sparse Core Ops, SparseCore 0:
  42.7 75.9 all-gather.2
where the time goes:
time: 164 us; the launch traced here: 163 us
  waiting for transfers between devices  84.1 us (51%)
  starting transfers between devices  32.8 us (20%)
  matrix products  26.8 us (16%)
  between operations  14 us (9%)
  other arithmetic  3.18 us (2%)
  local copies, waits for them, and re-layouts  1.76 us (1%)
    all_gather x1, waiting for transfers between devices, per_device(): piece = lax.all_gather(feat[None], 'peer', axis=0, tiled=True)  75.5 us
    ppermute x4, starting transfers between devices, extended(): lax.ppermute(head, axis, [((i + 1) % count, i) for i in range(ends)])  24.7 us
    dot_general x18, matrix products, apply_dilated_filter(): jnp.einsum('rwi,io->rwo', input_window, filter_kernel[kernel_tap_row, ker...  11.4 us
    dot_general x18, matrix products, apply_dilated_filter(): jnp.einsum('rwo,io->rwi', input_window, filter_kernel[2 - kernel_tap_row,...  9.54 us
    ppermute x4, starting transfers between devices, extended(): lax.ppermute(tail, axis, [(i, (i + 1) % count) for i in range(ends)])  8.08 us
    ppermute x4, waiting for transfers between devices, extended(): lax.ppermute(head, axis, [((i + 1) % count, i) for i in range(ends)])  7.33 us
    dot_general x1, matrix products, per_device(): jnp.einsum('k,krwc->rwc', pick, piece, preferred_element_type=jnp.float32)  5.87 us
  transfers between devices with their start and end apart: 9, of which 7 were waited for; matrix products, arithmetic and copies ran while one was open for 0% of the time, Pallas kernels for 0%

commit v1 on v0

v1 whole, which is shorter than its diff:
```python
import jax
import jax.numpy as jnp
from jax import lax
from jax.experimental import pallas as pl
from jax.experimental.pallas import tpu as pltpu
from jax.sharding import PartitionSpec as P

MESH = pl.DeviceIdType.MESH
BF16 = jnp.bfloat16
F32 = jnp.float32

ROWS = 16
COLS = 32
CH = 512
PEERS = 8
SPACE = 32
TAPS = 3
POS = ROWS * COLS


def sigmoid(value):
    return 0.5 + 0.5 * jnp.tanh(0.5 * value)


def span(first, count):
    return pl.ds(first * COLS, count * COLS)


def mul(left, right):
    return jnp.dot(left, right, preferred_element_type=F32)


def mul_t(left, right):
    return lax.dot_general(left, right, (((1,), (1,)), ((), ())), preferred_element_type=F32)


def put_shifted(buf, at, value, step):
    count = value.shape[0]
    col = lax.broadcasted_iota(jnp.int32, value.shape, 0) & (COLS - 1)
    ahead = jnp.where(col >= step, pltpu.roll(value, step, 0), 0.0)
    behind = jnp.where(col < COLS - step, pltpu.roll(value, count - step, 0), 0.0)
    buf[0, at, :] = ahead.astype(BF16)
    buf[2, at, :] = behind.astype(BF16)


def kernel(
    pairing,
    images,
    task_grad,
    first_kernel,
    first_scale,
    first_shift,
    second_kernel,
    second_scale,
    second_shift,
    out,
    w1,
    w2,
    img,
    hid,
    grad2,
    grad1,
    img_halo,
    hid_halo,
    grad2_halo,
    grad1_halo,
    pre1,
    pre2,
    acc,
    task,
    feat_in,
    feat_ed,
    spread_in,
    spread_ed,
    picked_in,
    picked_ed,
    partner_in,
    partner_ed,
    load_sem,
    w1_sem,
    w2_sem,
    halo_send,
    halo_recv,
    swap_send,
    swap_recv,
):
    peer = lax.axis_index("peer")
    place = lax.axis_index("space")
    half = SPACE // 2
    across = lax.rem(place + half, SPACE)
    after = lax.rem(place + 1, SPACE)
    before = lax.rem(place + SPACE - 1, SPACE)

    image_load = pltpu.make_async_copy(images.at[0], img.at[1, span(2, ROWS)], load_sem.at[0])
    image_load.start()
    w1_loads = [
        pltpu.make_async_copy(first_kernel.at[0, a], w1.at[a], w1_sem.at[a]) for a in range(TAPS)
    ]
    w2_loads = [
        pltpu.make_async_copy(second_kernel.at[0, a], w2.at[a], w2_sem.at[a]) for a in range(TAPS)
    ]
    task_load = pltpu.make_async_copy(task_grad.at[0], task, load_sem.at[1])
    for a in (1, 0, 2):
        w1_loads[a].start()

    barrier = pltpu.get_barrier_semaphore()
    for neighbour in (before, after):
        pl.semaphore_signal(barrier, inc=1, device_id=(peer, neighbour), device_id_type=MESH)
    for other in range(PEERS):
        pl.semaphore_signal(barrier, inc=1, device_id=(other, across), device_id_type=MESH)
    pl.semaphore_wait(barrier, 2 + PEERS)

    def halo_copies(stage, head, tail, landing):
        down = pltpu.make_async_remote_copy(
            src_ref=tail,
            dst_ref=landing.at[0],
            send_sem=halo_send.at[stage, 0],
            recv_sem=halo_recv.at[stage, 0],
            device_id=(peer, after),
            device_id_type=MESH,
        )
        up = pltpu.make_async_remote_copy(
            src_ref=head,
            dst_ref=landing.at[1],
            send_sem=halo_send.at[stage, 1],
            recv_sem=halo_recv.at[stage, 1],
            device_id=(peer, before),
            device_id_type=MESH,
        )
        return down, up

    def take_halo(buf, landing, step):
        for side, keep in ((0, place > 0), (1, place < SPACE - 1)):
            at = span(0 if side == 0 else ROWS + step, step)
            value = jnp.where(keep, landing[side].astype(F32), 0.0)
            buf[1, at, :] = value.astype(BF16)
            put_shifted(buf, at, value, step)

    def swap_copies(chunk, phase, source, landing):
        return [
            pltpu.make_async_remote_copy(
                src_ref=source.at[i],
                dst_ref=landing.at[peer],
                send_sem=swap_send.at[chunk, phase, i],
                recv_sem=swap_recv.at[chunk, phase, peer],
                device_id=(i, across),
                device_id_type=MESH,
            )
            for i in range(PEERS)
        ]

    def wait_swap(chunk, phase, source, landing):
        for i in range(PEERS):
            pltpu.make_async_remote_copy(
                src_ref=source.at[i],
                dst_ref=landing.at[i],
                send_sem=swap_send.at[chunk, phase, i],
                recv_sem=swap_recv.at[chunk, phase, i],
                device_id=(i, across),
                device_id_type=MESH,
            ).wait_recv()

    image_halo = halo_copies(0, img.at[1, span(2, 2)], img.at[1, span(ROWS, 2)], img_halo)
    image_load.wait()
    for copy in image_halo:
        copy.start()

    @pl.loop(0, ROWS // 2)
    def _(i):
        at = pl.ds(pl.multiple_of((i * 2 + 2) * COLS, 2 * COLS), 2 * COLS)
        put_shifted(img, at, img[1, at, :].astype(F32), 2)

    w1_loads[1].wait()
    acc[...] = sum(mul(img[b, span(2, ROWS)], w1[1, b]) for b in range(TAPS))
    for load in w2_loads:
        load.start()
    task_load.start()
    w1_loads[0].wait()
    w1_loads[2].wait()
    for copy in image_halo:
        copy.wait_recv()
    take_halo(img, img_halo, 2)
    acc[...] += sum(
        mul(img[b, span(2 * a, ROWS)], w1[a, b]) for a in (0, 2) for b in range(TAPS)
    )

    scale1 = first_scale[...]
    shift1 = first_shift[...]

    @pl.loop(0, ROWS // 2)
    def _(i):
        source = pl.ds(pl.multiple_of(i * 2 * COLS, 2 * COLS), 2 * COLS)
        at = pl.ds(pl.multiple_of((i * 2 + 4) * COLS, 2 * COLS), 2 * COLS)
        value = scale1 * acc[source, :] + shift1
        pre1[source, :] = value
        value = value * sigmoid(value)
        hid[1, at, :] = value.astype(BF16)
        put_shifted(hid, at, value, 4)

    hidden_halo = halo_copies(1, hid.at[1, span(4, 4)], hid.at[1, span(ROWS, 4)], hid_halo)
    for copy in hidden_halo:
        copy.start()

    for load in w2_loads:
        load.wait()
    scale2 = second_scale[...]
    shift2 = second_shift[...]

    acc[span(4, 8)] = sum(
        mul(hid[b, span(4 + 4 * a, 8)], w2[a, b]) for a in range(TAPS) for b in range(TAPS)
    )

    def features(row, piece_buf, piece):
        at = span(row, 1)
        value = scale2 * acc[at, :] + shift2
        pre2[at, :] = value
        piece_buf[piece] = (value * sigmoid(value)).astype(BF16)

    for i in range(PEERS):
        features(4 + i, feat_in, i)
    first_in = swap_copies(0, 0, feat_in, spread_in)
    for copy in first_in:
        copy.start()

    acc[span(0, 4)] = sum(
        mul(hid[b, span(4 * a, 4)], w2[a, b])
        for a, at in ((1, 4), (2, 8))
        for b in range(TAPS)
    )
    acc[span(12, 4)] = sum(
        mul(hid[b, span(12 + 4 * a, 4)], w2[a, b])
        for a in (0, 1)
        for b in range(TAPS)
    )
    for copy in hidden_halo:
        copy.wait_recv()
    take_halo(hid, hid_halo, 4)
    acc[span(0, 4)] += sum(mul(hid[b, span(0, 4)], w2[0, b]) for b in range(TAPS))
    acc[span(12, 4)] += sum(mul(hid[b, span(20, 4)], w2[2, b]) for b in range(TAPS))
    for i in range(PEERS):
        features(i if i < 4 else 8 + i, feat_ed, i)
    first_ed = swap_copies(1, 0, feat_ed, spread_ed)
    for copy in first_ed:
        copy.start()

    def slope(value):
        s = sigmoid(value)
        return s * (1.0 + value * (1.0 - s))

    @pl.loop(0, ROWS)
    def _(i):
        at = pl.ds(pl.multiple_of(i * COLS, COLS), COLS)
        pre1[at, :] = slope(pre1[at, :]) * scale1
        pre2[at, :] = slope(pre2[at, :]) * scale2

    task_load.wait()

    wait_swap(0, 0, feat_in, spread_in)
    for i in range(PEERS):
        picked_in[i] = spread_in[pairing[i]]
    second_in = swap_copies(0, 1, picked_in, partner_in)
    for copy in second_in:
        copy.start()
    wait_swap(1, 0, feat_ed, spread_ed)
    for i in range(PEERS):
        picked_ed[i] = spread_ed[pairing[i]]
    second_ed = swap_copies(1, 1, picked_ed, partner_ed)
    for copy in second_ed:
        copy.start()

    def cotangent(row, feat, partner, piece):
        at = span(row, 1)
        cot = task[row].astype(F32) + feat[piece].astype(F32) - partner[piece].astype(F32)
        value = cot * pre2[at, :]
        to = span(row + 4, 1)
        grad2[1, to, :] = value.astype(BF16)
        put_shifted(grad2, to, value, 4)

    def back2(first, count, a):
        return sum(
            mul_t(grad2[b, span(first + 4, count)], w2[2 - a, 2 - b]) for b in range(TAPS)
        )

    wait_swap(0, 1, picked_in, partner_in)
    for i in range(PEERS):
        cotangent(4 + i, feat_in, partner_in, i)
    acc[span(4, 8)] = back2(4, 8, 1)
    acc[span(0, 4)] = back2(4, 4, 2)
    acc[span(4, 4)] += back2(8, 4, 2)
    acc[span(12, 4)] = back2(8, 4, 0)
    acc[span(8, 4)] += back2(4, 4, 0)

    wait_swap(1, 1, picked_ed, partner_ed)
    for i in range(PEERS):
        cotangent(i if i < 4 else 8 + i, feat_ed, partner_ed, i)
    cot_halo = halo_copies(2, grad2.at[1, span(4, 4)], grad2.at[1, span(ROWS, 4)], grad2_halo)
    for copy in cot_halo:
        copy.start()
    acc[span(0, 4)] += back2(0, 4, 1)
    acc[span(12, 4)] += back2(12, 4, 1)
    acc[span(4, 4)] += back2(0, 4, 0)
    acc[span(8, 4)] += back2(12, 4, 2)
    for copy in cot_halo:
        copy.wait_recv()
    take_halo(grad2, grad2_halo, 4)
    acc[span(0, 4)] += back2(-4, 4, 0)
    acc[span(12, 4)] += back2(16, 4, 2)

    @pl.loop(0, ROWS // 2)
    def _(i):
        source = pl.ds(pl.multiple_of(i * 2 * COLS, 2 * COLS), 2 * COLS)
        at = pl.ds(pl.multiple_of((i * 2 + 2) * COLS, 2 * COLS), 2 * COLS)
        value = acc[source, :] * pre1[source, :]
        grad1[1, at, :] = value.astype(BF16)
        put_shifted(grad1, at, value, 2)

    hid_grad_halo = halo_copies(3, grad1.at[1, span(2, 2)], grad1.at[1, span(ROWS, 2)], grad1_halo)
    for copy in hid_grad_halo:
        copy.start()
    acc[...] = sum(mul_t(grad1[b, span(2, ROWS)], w1[1, 2 - b]) for b in range(TAPS))
    for copy in hid_grad_halo:
        copy.wait_recv()
    take_halo(grad1, grad1_halo, 2)
    out[0] = (
        acc[...]
        + sum(
            mul_t(grad1[b, span(2 * a, ROWS)], w1[2 - a, 2 - b])
            for a in (0, 2)
            for b in range(TAPS)
        )
    ).reshape(ROWS, COLS, CH).astype(BF16)

    for copies in (
        image_halo,
        hidden_halo,
        cot_halo,
        hid_grad_halo,
        first_in,
        first_ed,
        second_in,
        second_ed,
    ):
        for copy in copies:
            copy.wait_send()


def per_device(*args):
    any_spec = pl.BlockSpec(memory_space=pl.ANY)
    vmem = pl.BlockSpec(memory_space=pltpu.VMEM)
    dma = pltpu.SemaphoreType.DMA
    pieces = pltpu.VMEM((PEERS, COLS, CH), BF16)
    return pl.pallas_call(
        kernel,
        out_shape=jax.ShapeDtypeStruct((1, ROWS, COLS, CH), BF16),
        in_specs=[
            pl.BlockSpec(memory_space=pltpu.SMEM),
            any_spec,
            any_spec,
            any_spec,
            vmem,
            vmem,
            any_spec,
            vmem,
            vmem,
        ],
        out_specs=vmem,
        scratch_shapes=[
            pltpu.VMEM((TAPS, TAPS, CH, CH), BF16),
            pltpu.VMEM((TAPS, TAPS, CH, CH), BF16),
            pltpu.VMEM((TAPS, (ROWS + 4) * COLS, CH), BF16),
            pltpu.VMEM((TAPS, (ROWS + 8) * COLS, CH), BF16),
            pltpu.VMEM((TAPS, (ROWS + 8) * COLS, CH), BF16),
            pltpu.VMEM((TAPS, (ROWS + 4) * COLS, CH), BF16),
            pltpu.VMEM((2, 2 * COLS, CH), BF16),
            pltpu.VMEM((2, 4 * COLS, CH), BF16),
            pltpu.VMEM((2, 4 * COLS, CH), BF16),
            pltpu.VMEM((2, 2 * COLS, CH), BF16),
            pltpu.VMEM((POS, CH), F32),
            pltpu.VMEM((POS, CH), F32),
            pltpu.VMEM((POS, CH), F32),
            pltpu.VMEM((ROWS, COLS, CH), BF16),
            pieces,
            pieces,
            pieces,
            pieces,
            pieces,
            pieces,
            pieces,
            pieces,
            dma((2,)),
            dma((TAPS,)),
            dma((TAPS,)),
            dma((4, 2)),
            dma((4, 2)),
            dma((2, 2, PEERS)),
            dma((2, 2, PEERS)),
        ],
        compiler_params=pltpu.CompilerParams(
            collective_id=0, has_side_effects=True, vmem_limit_bytes=56 << 20
        ),
        name="distill",
    )(args[2], args[0].reshape(1, POS, CH), args[1], *args[3:])


def solution(mesh):
    placed = (
        P("peer", "space", None, None),
        P("peer", "space", None, None),
        P(),
        P("peer", None, None, None, None),
        P("peer", None),
        P("peer", None),
        P("peer", None, None, None, None),
        P("peer", None),
        P("peer", None),
    )
    return jax.shard_map(
        per_device,
        mesh=mesh,
        in_specs=placed,
        out_specs=P("peer", "space", None, None),
        check_vma=False,
    )
```

time: 164 us -> 46.7 us (0.28)
  waiting for transfers between devices: 84.1 us -> 0 us
  Pallas kernels: 0 us -> 44.7 us
  starting transfers between devices: 32.8 us -> 0 us
  matrix products: 26.8 us -> 0 us
  between operations: 14 us -> 0.01 us
  other arithmetic: 3.18 us -> 0 us
    all_gather x1 -> x0, waiting for transfers between devices: 75.5 us -> none  [per_device(): piece = lax.all_gather(feat[None], 'peer', axis=0, tiled=True)]
    pallas_call x0 -> x1, Pallas kernels: none -> 44.7 us  [per_device(): pl.pallas_call(kernel, out_shape=jax.ShapeDtypeStruct((1, ROWS, COLS, CH)...]
    ppermute x8 -> x0, starting transfers between devices: 32.8 us -> none  [the longest x4 24.7 us: extended(): lax.ppermute(head, axis, [((i + 1) % count, i) for i in range(ends)])]
    dot_general x37 -> x0, matrix products: 26.8 us -> none  [the longest x18 11.4 us: apply_dilated_filter(): jnp.einsum('rwi,io->rwo', input_window, filter_kernel[kernel_tap_row, ker...]
    ppermute x8 -> x0, waiting for transfers between devices: 8.58 us -> none  [the longest x4 7.33 us: extended(): lax.ppermute(head, axis, [((i + 1) % count, i) for i in range(ends)])]
    concatenate x4 -> x0, other arithmetic: 2.6 us -> none  [extended(): jnp.concatenate([lax.ppermute(tail, axis, [(i, (i + 1) % count) for i in...]
    unnamed x28 -> x1, local copies, waits for them, and re-layouts: 0.09 us -> 1.88 us
  transfers between devices with their start and end apart: 9 -> 0, of which waited for: 7 -> 0; matrix products, arithmetic and copies ran while one was open for 0% -> 0% of each run, Pallas kernels for 0% -> 0%
where the time goes in v1:
time: 46.7 us; the launch traced here: 46.5 us
  Pallas kernels  44.7 us (96%)
  local copies, waits for them, and re-layouts  1.88 us (4%)
    pallas_call x1, Pallas kernels, per_device(): pl.pallas_call(kernel, out_shape=jax.ShapeDtypeStruct((1, ROWS, COLS, CH)...  44.7 us
    unnamed x1, local copies, waits for them, and re-layouts  1.88 us

profile of v1, /device:TPU:8, one launch (start us, length us, event | category | flops | bytes accessed | tf_op | source)
XLA Modules:
  0.0 46.5 jit_solution(13377412811794313243)
XLA Ops:
  0.0 44.7 %distill.1 = bf16[1,16,32,512]{3,2,1,0:T(8,128)(2,1)} custom-call(s32[8]{0:T(128)} %pairing.1, bf16[1,512,512]{2,1,0:T(8,128)(2,1)} %bitcast.1, bf16[1,16,32,512]{3,2,1,0:T(8,128)(2,1)} %task_grad.1, bf16[1,3,3,512,512]{4,3,2,1,0:T(8,128)(2,1)} %first_kernel.1, f32[1,512]{1,0:T(1,128)} %first_scale.1, f32[1,512]{1,0:T(1,128)} %first_shift.1, ...), custom_call_target="tpu_custom_call" | custom-call | tf_op jit(solution)/shard_map/distill/pallas_call | solution.py:352
  44.7 1.9 %copy.11 = bf16[1,16,32,512]{3,2,1,0:T(8,128)(2,1)} copy(bf16[1,16,32,512]{3,2,1,0:T(8,128)(2,1)} %distill.1) | data formatting | bytes 1048576

commit v2 on v0

v2 whole, which is shorter than its diff:
```python
import jax
import jax.numpy as jnp
from jax import lax
from jax.experimental import pallas as pl
from jax.experimental.pallas import tpu as pltpu
from jax.sharding import PartitionSpec as P

MESH = pl.DeviceIdType.MESH
BF16 = jnp.bfloat16
F32 = jnp.float32

ROWS = 16
COLS = 32
CH = 512
PEERS = 8
SPACE = 32
TAPS = 3
POS = ROWS * COLS
HALF = CH // 2
EDGE = (0, 1, 2, 3, 12, 13, 14, 15)
INNER = tuple(range(4, 12))
LANES = (pl.ds(0, HALF), pl.ds(HALF, HALF))
CHUNKS = ((INNER, 0), (INNER, 1), (EDGE, 0), (EDGE, 1))


def sigmoid(value):
    return 0.5 + 0.5 * jnp.tanh(0.5 * value)


def span(first, count):
    return pl.ds(first * COLS, count * COLS)


def mul(left, right):
    return jnp.dot(left, right, preferred_element_type=F32)


def mul_t(left, right):
    return lax.dot_general(left, right, (((1,), (1,)), ((), ())), preferred_element_type=F32)


def put_shifted(buf, at, value, step, lanes=slice(None)):
    count = value.shape[0]
    col = lax.broadcasted_iota(jnp.int32, value.shape, 0) & (COLS - 1)
    ahead = jnp.where(col >= step, pltpu.roll(value, step, 0), 0.0)
    behind = jnp.where(col < COLS - step, pltpu.roll(value, count - step, 0), 0.0)
    buf[0, at, lanes] = ahead.astype(BF16)
    buf[2, at, lanes] = behind.astype(BF16)


def kernel(
    pairing_in,
    images,
    task_grad,
    first_kernel,
    first_scale,
    first_shift,
    second_kernel,
    second_scale,
    second_shift,
    out,
    pairing,
    norms,
    w1,
    w2,
    img,
    hid,
    grad2,
    grad1,
    img_halo,
    hid_halo,
    grad2_halo_a,
    grad2_halo_b,
    grad1_halo,
    pre1,
    pre2,
    acc,
    task,
    *rest,
):
    feat, spread, picked, partner = (rest[4 * i : 4 * i + 4] for i in range(4))
    load_sem, w1_sem, w2_sem, halo_send, halo_recv, swap_send, swap_recv = rest[16:]
    peer = lax.axis_index("peer")
    place = lax.axis_index("space")
    across = lax.rem(place + SPACE // 2, SPACE)
    after = lax.rem(place + 1, SPACE)
    before = lax.rem(place + SPACE - 1, SPACE)
    has_after = place < SPACE - 1
    has_before = place > 0

    image_load = pltpu.make_async_copy(images.at[0], img.at[1, span(2, ROWS)], load_sem.at[0])
    image_load.start()
    w1_loads = [
        pltpu.make_async_copy(first_kernel.at[0, a], w1.at[a], w1_sem.at[a]) for a in range(TAPS)
    ]
    w2_loads = [
        pltpu.make_async_copy(second_kernel.at[0, a], w2.at[a], w2_sem.at[a]) for a in range(TAPS)
    ]
    task_load = pltpu.make_async_copy(task_grad.at[0], task, load_sem.at[1])
    for a in (1, 0, 2):
        w1_loads[a].start()
    small_loads = [
        pltpu.make_async_copy(array, norms.at[i], load_sem.at[2 + i])
        for i, array in enumerate((first_scale, first_shift, second_scale, second_shift))
    ]
    small_loads.append(pltpu.make_async_copy(pairing_in, pairing, load_sem.at[6]))
    for load in small_loads:
        load.start()

    barrier = pltpu.get_barrier_semaphore()
    for neighbour in (before, after):
        pl.semaphore_signal(barrier, inc=1, device_id=(peer, neighbour), device_id_type=MESH)
    for other in range(PEERS):
        pl.semaphore_signal(barrier, inc=1, device_id=(other, across), device_id_type=MESH)

    landings = (img_halo, hid_halo, grad2_halo_a, grad2_halo_b, grad1_halo)
    for side, missing in ((0, place == 0), (1, place == SPACE - 1)):

        @pl.when(missing)
        def _(side=side):
            for landing in landings:
                landing[side] = jnp.zeros(landing.shape[1:], BF16)

    pl.semaphore_wait(barrier, 2 + PEERS)

    def halo_copies(stage, head, tail):
        down = pltpu.make_async_remote_copy(
            src_ref=tail,
            dst_ref=landings[stage].at[0],
            send_sem=halo_send.at[stage, 0],
            recv_sem=halo_recv.at[stage, 0],
            device_id=(peer, after),
            device_id_type=MESH,
        )
        up = pltpu.make_async_remote_copy(
            src_ref=head,
            dst_ref=landings[stage].at[1],
            send_sem=halo_send.at[stage, 1],
            recv_sem=halo_recv.at[stage, 1],
            device_id=(peer, before),
            device_id_type=MESH,
        )

        @pl.when(has_after)
        def _():
            down.start()

        @pl.when(has_before)
        def _():
            up.start()

        return down, up

    def wait_halo(copies):
        down, up = copies

        @pl.when(has_before)
        def _():
            down.wait_recv()

        @pl.when(has_after)
        def _():
            up.wait_recv()

    def take_halo(buf, stage, step, lanes=slice(None)):
        for side in (0, 1):
            at = span(0 if side == 0 else ROWS + step, step)
            value = landings[stage][side]
            buf[1, at, lanes] = value
            put_shifted(buf, at, value.astype(F32), step, lanes)

    def swap_copy(chunk, phase, source, landing, i, slot):
        return pltpu.make_async_remote_copy(
            src_ref=source[chunk].at[i],
            dst_ref=landing[chunk].at[slot],
            send_sem=swap_send.at[chunk, phase, i],
            recv_sem=swap_recv.at[chunk, phase, slot],
            device_id=(i, across),
            device_id_type=MESH,
        )

    def send_pieces(chunk, phase):
        source, landing = ((feat, spread), (picked, partner))[phase]
        for i in range(PEERS):
            swap_copy(chunk, phase, source, landing, i, peer).start()

    def wait_pieces(chunk, phase):
        source, landing = ((feat, spread), (picked, partner))[phase]
        for i in range(PEERS):
            swap_copy(chunk, phase, source, landing, i, i).wait_recv()

    image_halo = halo_copies(0, images.at[0, span(0, 2)], images.at[0, span(ROWS - 2, 2)])

    image_load.wait()

    @pl.loop(0, ROWS // 2)
    def _(i):
        at = pl.ds(pl.multiple_of((i * 2 + 2) * COLS, 2 * COLS), 2 * COLS)
        put_shifted(img, at, img[1, at, :].astype(F32), 2)

    w1_loads[1].wait()
    acc[...] = sum(mul(img[b, span(2, ROWS)], w1[1, b]) for b in range(TAPS))
    for load in w2_loads:
        load.start()
    task_load.start()
    w1_loads[0].wait()
    acc[span(2, ROWS - 2)] += sum(mul(img[b, span(2, ROWS - 2)], w1[0, b]) for b in range(TAPS))
    w1_loads[2].wait()
    acc[span(0, ROWS - 2)] += sum(mul(img[b, span(4, ROWS - 2)], w1[2, b]) for b in range(TAPS))

    for load in small_loads:
        load.wait()
    scale1, shift1, scale2, shift2 = (norms[i] for i in range(4))

    def hidden_rows(first, count):
        @pl.loop(0, count // 2)
        def _(i):
            source = pl.ds(pl.multiple_of((first + i * 2) * COLS, 2 * COLS), 2 * COLS)
            at = pl.ds(pl.multiple_of((first + i * 2 + 4) * COLS, 2 * COLS), 2 * COLS)
            value = scale1 * acc[source, :] + shift1
            pre1[source, :] = value
            value = value * sigmoid(value)
            hid[1, at, :] = value.astype(BF16)
            put_shifted(hid, at, value, 4)

    hidden_rows(4, 8)
    wait_halo(image_halo)
    take_halo(img, 0, 2)
    acc[span(0, 2)] += sum(mul(img[b, span(0, 2)], w1[0, b]) for b in range(TAPS))
    acc[span(ROWS - 2, 2)] += sum(mul(img[b, span(ROWS + 2, 2)], w1[2, b]) for b in range(TAPS))
    hidden_rows(0, 4)
    hidden_rows(12, 4)
    hidden_halo = halo_copies(1, hid.at[1, span(4, 4)], hid.at[1, span(ROWS, 4)])

    for load in w2_loads:
        load.wait()

    def features(chunk):
        rows, half = CHUNKS[chunk]
        lanes = LANES[half]
        scale = scale2[:, half * HALF : (half + 1) * HALF]
        shift = shift2[:, half * HALF : (half + 1) * HALF]
        for i, row in enumerate(rows):
            at = span(row, 1)
            value = scale * acc[at, lanes] + shift
            pre2[at, lanes] = value
            feat[chunk][i] = (value * sigmoid(value)).astype(BF16)
        send_pieces(chunk, 0)

    for half in (0, 1):
        acc[span(4, 8), LANES[half]] = sum(
            mul(hid[b, span(4 + 4 * a, 8)], w2[a, b, :, LANES[half]])
            for a in range(TAPS)
            for b in range(TAPS)
        )
        features(half)

    middle = sum(
        mul(jnp.concatenate([hid[b, span(4, 4)], hid[b, span(16, 4)]], 0), w2[1, b])
        for b in range(TAPS)
    )
    acc[span(0, 4)] = middle[: POS // 4]
    acc[span(12, 4)] = middle[POS // 4 :]
    acc[span(0, 4)] += sum(mul(hid[b, span(8, 4)], w2[2, b]) for b in range(TAPS))
    acc[span(12, 4)] += sum(mul(hid[b, span(12, 4)], w2[0, b]) for b in range(TAPS))
    wait_halo(hidden_halo)
    take_halo(hid, 1, 4)
    for half in (0, 1):
        for row, at, a in ((0, 0, 0), (12, 20, 2)):
            acc[span(row, 4), LANES[half]] += sum(
                mul(hid[b, span(at, 4)], w2[a, b, :, LANES[half]]) for b in range(TAPS)
            )
        features(2 + half)

    def slope(value):
        s = sigmoid(value)
        return s * (1.0 + value * (1.0 - s))

    @pl.loop(0, ROWS)
    def _(i):
        at = pl.ds(pl.multiple_of(i * COLS, COLS), COLS)
        pre2[at, :] = slope(pre2[at, :]) * scale2
        pre1[at, :] = slope(pre1[at, :]) * scale1

    task_load.wait()

    def pass_on(chunk):
        wait_pieces(chunk, 0)
        for i in range(PEERS):
            picked[chunk][i] = spread[chunk][pairing[i]]
        send_pieces(chunk, 1)

    for chunk in (2, 3, 0, 1):
        pass_on(chunk)

    def cotangent(chunk):
        rows, half = CHUNKS[chunk]
        lanes = LANES[half]
        wait_pieces(chunk, 1)
        for i, row in enumerate(rows):
            cot = task[row, :, lanes].astype(F32) + feat[chunk][i].astype(F32)
            value = (cot - partner[chunk][i].astype(F32)) * pre2[span(row, 1), lanes]
            to = span(row + 4, 1)
            grad2[1, to, lanes] = value.astype(BF16)
            put_shifted(grad2, to, value, 4, lanes)

    def back2(first, count, a, half):
        lanes = LANES[half]
        return sum(
            mul_t(grad2[b, span(first + 4, count), lanes], w2[2 - a, 2 - b, :, lanes])
            for b in range(TAPS)
        )

    cot_halo = []
    for half in (0, 1):
        lanes = LANES[half]
        cotangent(2 + half)
        cot_halo.append(
            halo_copies(
                2 + half, grad2.at[1, span(4, 4), lanes], grad2.at[1, span(ROWS, 4), lanes]
            )
        )
        middle = sum(
            mul_t(
                jnp.concatenate([grad2[b, span(4, 4), lanes], grad2[b, span(16, 4), lanes]], 0),
                w2[1, 2 - b, :, lanes],
            )
            for b in range(TAPS)
        )
        if half == 0:
            acc[span(0, 4)] = middle[: POS // 4]
            acc[span(12, 4)] = middle[POS // 4 :]
            acc[span(4, 4)] = back2(0, 4, 0, half)
            acc[span(8, 4)] = back2(12, 4, 2, half)
        else:
            acc[span(0, 4)] += middle[: POS // 4]
            acc[span(12, 4)] += middle[POS // 4 :]
            acc[span(4, 4)] += back2(0, 4, 0, half)
            acc[span(8, 4)] += back2(12, 4, 2, half)

    def inner_back2(half):
        acc[span(4, 8)] += back2(4, 8, 1, half)
        acc[span(0, 8)] += back2(4, 8, 2, half)
        acc[span(8, 8)] += back2(4, 8, 0, half)

    cotangent(0)
    inner_back2(0)
    for half in (0, 1):
        wait_halo(cot_halo[half])
        take_halo(grad2, 2 + half, 4, LANES[half])
        acc[span(0, 4)] += back2(-4, 4, 0, half)
        acc[span(12, 4)] += back2(16, 4, 2, half)
    cotangent(1)
    inner_back2(1)

    def grad1_rows(first, count):
        @pl.loop(0, count // 2)
        def _(i):
            source = pl.ds(pl.multiple_of((first + i * 2) * COLS, 2 * COLS), 2 * COLS)
            at = pl.ds(pl.multiple_of((first + i * 2 + 2) * COLS, 2 * COLS), 2 * COLS)
            value = acc[source, :] * pre1[source, :]
            grad1[1, at, :] = value.astype(BF16)
            put_shifted(grad1, at, value, 2)

    grad1_rows(0, 2)
    grad1_rows(ROWS - 2, 2)
    hid_grad_halo = halo_copies(4, grad1.at[1, span(2, 2)], grad1.at[1, span(ROWS, 2)])
    grad1_rows(2, ROWS - 4)

    def back1(first, count, a):
        return sum(
            mul_t(grad1[b, span(first + 2, count)], w1[2 - a, 2 - b]) for b in range(TAPS)
        )

    acc[...] = back1(0, ROWS, 1)
    acc[span(2, ROWS - 2)] += back1(0, ROWS - 2, 0)
    acc[span(0, ROWS - 2)] += back1(2, ROWS - 2, 2)
    out[0, 2 : ROWS - 2] = acc[span(2, ROWS - 4)].reshape(ROWS - 4, COLS, CH).astype(BF16)
    wait_halo(hid_grad_halo)
    take_halo(grad1, 4, 2)
    out[0, 0:2] = (acc[span(0, 2)] + back1(-2, 2, 0)).reshape(2, COLS, CH).astype(BF16)
    out[0, ROWS - 2 :] = (
        (acc[span(ROWS - 2, 2)] + back1(ROWS, 2, 2)).reshape(2, COLS, CH).astype(BF16)
    )

    for down, up in (image_halo, hidden_halo, *cot_halo, hid_grad_halo):

        @pl.when(has_after)
        def _(down=down):
            down.wait_send()

        @pl.when(has_before)
        def _(up=up):
            up.wait_send()

    for phase, source, landing in ((0, feat, spread), (1, picked, partner)):
        for chunk in range(4):
            for i in range(PEERS):
                swap_copy(chunk, phase, source, landing, i, peer).wait_send()


def per_device(*args):
    hbm = pl.BlockSpec(memory_space=pltpu.HBM)
    vmem = pl.BlockSpec(memory_space=pltpu.VMEM)
    dma = pltpu.SemaphoreType.DMA
    pieces = pltpu.VMEM((PEERS, COLS, HALF), BF16)
    return pl.pallas_call(
        kernel,
        out_shape=jax.ShapeDtypeStruct((1, ROWS, COLS, CH), BF16),
        in_specs=[hbm] * 9,
        out_specs=vmem,
        scratch_shapes=[
            pltpu.SMEM((PEERS,), jnp.int32),
            pltpu.VMEM((4, 1, CH), F32),
            pltpu.VMEM((TAPS, TAPS, CH, CH), BF16),
            pltpu.VMEM((TAPS, TAPS, CH, CH), BF16),
            pltpu.VMEM((TAPS, (ROWS + 4) * COLS, CH), BF16),
            pltpu.VMEM((TAPS, (ROWS + 8) * COLS, CH), BF16),
            pltpu.VMEM((TAPS, (ROWS + 8) * COLS, CH), BF16),
            pltpu.VMEM((TAPS, (ROWS + 4) * COLS, CH), BF16),
            pltpu.VMEM((2, 2 * COLS, CH), BF16),
            pltpu.VMEM((2, 4 * COLS, CH), BF16),
            pltpu.VMEM((2, 4 * COLS, HALF), BF16),
            pltpu.VMEM((2, 4 * COLS, HALF), BF16),
            pltpu.VMEM((2, 2 * COLS, CH), BF16),
            pltpu.VMEM((POS, CH), F32),
            pltpu.VMEM((POS, CH), F32),
            pltpu.VMEM((POS, CH), F32),
            pltpu.VMEM((ROWS, COLS, CH), BF16),
            *[pieces] * 16,
            dma((7,)),
            dma((TAPS,)),
            dma((TAPS,)),
            dma((5, 2)),
            dma((5, 2)),
            dma((4, 2, PEERS)),
            dma((4, 2, PEERS)),
        ],
        compiler_params=pltpu.CompilerParams(
            collective_id=0, has_side_effects=True, vmem_limit_bytes=34 << 20
        ),
        name="distill",
    )(
        *(
            pltpu.with_memory_space_constraint(x, pltpu.HBM)
            for x in (args[2], args[0].reshape(1, POS, CH), args[1], *args[3:])
        )
    )


def solution(mesh):
    placed = (
        P("peer", "space", None, None),
        P("peer", "space", None, None),
        P(),
        P("peer", None, None, None, None),
        P("peer", None),
        P("peer", None),
        P("peer", None, None, None, None),
        P("peer", None),
        P("peer", None),
    )
    return jax.shard_map(
        per_device,
        mesh=mesh,
        in_specs=placed,
        out_specs=P("peer", "space", None, None),
        check_vma=False,
    )
```

time: 164 us -> 41.1 us (0.25)
  waiting for transfers between devices: 84.1 us -> 0 us
  Pallas kernels: 0 us -> 40.2 us
  starting transfers between devices: 32.8 us -> 0 us
  matrix products: 26.8 us -> 0 us
  between operations: 14 us -> 0.01 us
  other arithmetic: 3.18 us -> 0 us
    all_gather x1 -> x0, waiting for transfers between devices: 75.5 us -> none  [per_device(): piece = lax.all_gather(feat[None], 'peer', axis=0, tiled=True)]
    pallas_call x0 -> x1, Pallas kernels: none -> 40.2 us  [per_device(): pl.pallas_call(kernel, out_shape=jax.ShapeDtypeStruct((1, ROWS, COLS, CH)...]
    ppermute x8 -> x0, starting transfers between devices: 32.8 us -> none  [the longest x4 24.7 us: extended(): lax.ppermute(head, axis, [((i + 1) % count, i) for i in range(ends)])]
    dot_general x37 -> x0, matrix products: 26.8 us -> none  [the longest x18 11.4 us: apply_dilated_filter(): jnp.einsum('rwi,io->rwo', input_window, filter_kernel[kernel_tap_row, ker...]
    ppermute x8 -> x0, waiting for transfers between devices: 8.58 us -> none  [the longest x4 7.33 us: extended(): lax.ppermute(head, axis, [((i + 1) % count, i) for i in range(ends)])]
    concatenate x4 -> x0, other arithmetic: 2.6 us -> none  [extended(): jnp.concatenate([lax.ppermute(tail, axis, [(i, (i + 1) % count) for i in...]
  transfers between devices with their start and end apart: 9 -> 0, of which waited for: 7 -> 0; matrix products, arithmetic and copies ran while one was open for 0% -> 0% of each run, Pallas kernels for 0% -> 0%
where the time goes in v2:
time: 41.1 us; the launch traced here: 41 us
  Pallas kernels  40.2 us (98%)
  local copies, waits for them, and re-layouts  0.8 us (2%)
    pallas_call x1, Pallas kernels, per_device(): pl.pallas_call(kernel, out_shape=jax.ShapeDtypeStruct((1, ROWS, COLS, CH)...  40.2 us

profile of v2, /device:TPU:8, one launch (start us, length us, event | category | flops | bytes accessed | tf_op | source)
XLA Modules:
  0.0 41.0 jit_solution(10940974174516042724)
XLA Ops:
  0.0 40.2 %distill.1 = bf16[1,16,32,512]{3,2,1,0:T(8,128)(2,1)S(1)} custom-call(s32[8]{0:T(128)} %pairing_in.1, bf16[1,512,512]{2,1,0:T(8,128)(2,1)} %bitcast.1, bf16[1,16,32,512]{3,2,1,0:T(8,128)(2,1)} %task_grad.1, bf16[1,3,3,512,512]{4,3,2,1,0:T(8,128)(2,1)} %first_kernel.1, f32[1,512]{1,0:T(1,128)} %first_scale.1, f32[1,512]{1,0:T(1,128)} %first_shift.1, ...), custom_call_target="tpu_custom_call" | custom-call | tf_op jit(solution)/shard_map/distill/pallas_call | solution.py:407
  40.2 0.8 %copy.11 = bf16[1,16,32,512]{3,2,1,0:T(8,128)(2,1)} copy(bf16[1,16,32,512]{3,2,1,0:T(8,128)(2,1)S(1)} %distill.1) | data formatting | bytes 1048576

commit v3 on v2

--- a/solution.py
+++ b/solution.py
@@ -193,7 +193,7 @@
 
     image_load.wait()
 
-    @pl.loop(0, ROWS // 2)
+    @pl.loop(0, ROWS // 2, unroll=True)
     def _(i):
         at = pl.ds(pl.multiple_of((i * 2 + 2) * COLS, 2 * COLS), 2 * COLS)
         put_shifted(img, at, img[1, at, :].astype(F32), 2)
@@ -213,7 +213,7 @@
     scale1, shift1, scale2, shift2 = (norms[i] for i in range(4))
 
     def hidden_rows(first, count):
-        @pl.loop(0, count // 2)
+        @pl.loop(0, count // 2, unroll=True)
         def _(i):
             source = pl.ds(pl.multiple_of((first + i * 2) * COLS, 2 * COLS), 2 * COLS)
             at = pl.ds(pl.multiple_of((first + i * 2 + 4) * COLS, 2 * COLS), 2 * COLS)
@@ -345,16 +345,16 @@
 
     cotangent(0)
     inner_back2(0)
+    cotangent(1)
+    inner_back2(1)
     for half in (0, 1):
         wait_halo(cot_halo[half])
         take_halo(grad2, 2 + half, 4, LANES[half])
         acc[span(0, 4)] += back2(-4, 4, 0, half)
         acc[span(12, 4)] += back2(16, 4, 2, half)
-    cotangent(1)
-    inner_back2(1)
 
     def grad1_rows(first, count):
-        @pl.loop(0, count // 2)
+        @pl.loop(0, count // 2, unroll=True)
         def _(i):
             source = pl.ds(pl.multiple_of((first + i * 2) * COLS, 2 * COLS), 2 * COLS)
             at = pl.ds(pl.multiple_of((first + i * 2 + 2) * COLS, 2 * COLS), 2 * COLS)

time: 41.1 us -> 40.7 us (level)
    pallas_call x1, Pallas kernels: 40.2 us -> 39.8 us  [per_device(): pl.pallas_call(kernel, out_shape=jax.ShapeDtypeStruct((1, ROWS, COLS, CH)...]
where the time goes in v3:
time: 40.7 us; the launch traced here: 40.6 us
  Pallas kernels  39.8 us (98%)
  local copies, waits for them, and re-layouts  0.8 us (2%)
    pallas_call x1, Pallas kernels, per_device(): pl.pallas_call(kernel, out_shape=jax.ShapeDtypeStruct((1, ROWS, COLS, CH)...  39.8 us

profile of v3, /device:TPU:8, one launch (start us, length us, event | category | flops | bytes accessed | tf_op | source)
XLA Modules:
  0.0 40.6 jit_solution(12550423430289723980)
XLA Ops:
  0.0 39.8 %distill.1 = bf16[1,16,32,512]{3,2,1,0:T(8,128)(2,1)S(1)} custom-call(s32[8]{0:T(128)} %pairing_in.1, bf16[1,512,512]{2,1,0:T(8,128)(2,1)} %bitcast.1, bf16[1,16,32,512]{3,2,1,0:T(8,128)(2,1)} %task_grad.1, bf16[1,3,3,512,512]{4,3,2,1,0:T(8,128)(2,1)} %first_kernel.1, f32[1,512]{1,0:T(1,128)} %first_scale.1, f32[1,512]{1,0:T(1,128)} %first_shift.1, ...), custom_call_target="tpu_custom_call" | custom-call | tf_op jit(solution)/shard_map/distill/pallas_call | solution.py:407
  39.8 0.8 %copy.11 = bf16[1,16,32,512]{3,2,1,0:T(8,128)(2,1)} copy(bf16[1,16,32,512]{3,2,1,0:T(8,128)(2,1)S(1)} %distill.1) | data formatting | bytes 1048576

commit v4 on v3

--- a/solution.py
+++ b/solution.py
@@ -290,7 +290,7 @@
             picked[chunk][i] = spread[chunk][pairing[i]]
         send_pieces(chunk, 1)
 
-    for chunk in (2, 3, 0, 1):
+    for chunk in (0, 2, 3, 1):
         pass_on(chunk)
 
     def cotangent(chunk):

time: 40.7 us -> 40.1 us (0.985)
  Pallas kernels: 39.8 us -> 39.2 us
    pallas_call x1, Pallas kernels: 39.8 us -> 39.2 us  [per_device(): pl.pallas_call(kernel, out_shape=jax.ShapeDtypeStruct((1, ROWS, COLS, CH)...]
where the time goes in v4:
time: 40.1 us; the launch traced here: 40 us
  Pallas kernels  39.2 us (98%)
  local copies, waits for them, and re-layouts  0.8 us (2%)
    pallas_call x1, Pallas kernels, per_device(): pl.pallas_call(kernel, out_shape=jax.ShapeDtypeStruct((1, ROWS, COLS, CH)...  39.2 us

profile of v4, /device:TPU:8, one launch (start us, length us, event | category | flops | bytes accessed | tf_op | source)
XLA Modules:
  0.0 40.0 jit_solution(7474102887114336197)
XLA Ops:
  0.0 39.2 %distill.1 = bf16[1,16,32,512]{3,2,1,0:T(8,128)(2,1)S(1)} custom-call(s32[8]{0:T(128)} %pairing_in.1, bf16[1,512,512]{2,1,0:T(8,128)(2,1)} %bitcast.1, bf16[1,16,32,512]{3,2,1,0:T(8,128)(2,1)} %task_grad.1, bf16[1,3,3,512,512]{4,3,2,1,0:T(8,128)(2,1)} %first_kernel.1, f32[1,512]{1,0:T(1,128)} %first_scale.1, f32[1,512]{1,0:T(1,128)} %first_shift.1, ...), custom_call_target="tpu_custom_call" | custom-call | tf_op jit(solution)/shard_map/distill/pallas_call | solution.py:407
  39.2 0.8 %copy.11 = bf16[1,16,32,512]{3,2,1,0:T(8,128)(2,1)} copy(bf16[1,16,32,512]{3,2,1,0:T(8,128)(2,1)S(1)} %distill.1) | data formatting | bytes 1048576
